TPU v7x, 32 devices: a whole 2x2x4 slice. The times are simulated.
32 devices in a mesh: rep: 8 (over z, y), grp: 4 (over x, core).
Axes of the slice: x: 2, y: 2, z: 4, core: 2. Of those that a mesh axis runs over, the one named last changes fastest.
Arguments:
- latents: bfloat16 [32768, 384], P(('rep', 'grp')), may hold values from -6 to 6
- condition: float32 [32, 384], P(('rep', 'grp')), may hold values from -6 to 6
- out_grad: bfloat16 [32768, 384], P(('rep', 'grp')), may hold values from -6 to 6
- master: float32 [20736, 128], P('grp')
- moment_one: float32 [20736, 128], P('grp'), may hold values from -512 to 512
- moment_two: float32 [20736, 128], P('grp'), may hold values from 1638 to 16384
- bias_master: float32 [5760], P('grp'), may hold values from -3 to 3
- bias_one: float32 [5760], P('grp'), may hold values from -512 to 512
- bias_two: float32 [5760], P('grp'), may hold values from 1638 to 16384
Outputs:
- block_out: bfloat16 [32768, 384], P(('rep', 'grp'))
- latent_grad: bfloat16 [32768, 384], P(('rep', 'grp'))
- condition_grad: float32 [32, 384], P(('rep', 'grp'))
- lamb_stats: float32 [3, 5], replicated
- new_master: float32 [20736, 128], P('grp')
- new_moment_one: float32 [20736, 128], P('grp')
- new_moment_two: float32 [20736, 128], P('grp')
- master_copy: bfloat16 [20736, 128], P('grp')
- new_bias: float32 [5760], P('grp')
- new_bias_one: float32 [5760], P('grp')
- new_bias_two: float32 [5760], P('grp')
- bias_copy: bfloat16 [5760], P('grp')
All inputs are finite; a program needn't handle non-finite values.
Results may differ from a plain program's by a relative error of at most 0.0095.
The roundings to bfloat16 on the way count: a program that leaves them out, or rounds other values in their place, can miss the bound.
Values may be sent and summed in bfloat16 or wider, within the bound.
A program may use at most 128 MiB of HBM per device.

v0:
```python
import functools

import jax
import jax.numpy as jnp
from jax import lax
from jax.experimental import pallas as pl
from jax.experimental.pallas import tpu as pltpu
from jax.sharding import PartitionSpec as P

D = 384
FF = 1536
HEADS = 6
HDIM = 64
PAIRS = HEADS // 2

NORM_EPS = 1e-06
BETA_ONE = 0.5
BETA_TWO = 0.5
ADAM_EPS = 1e-06
STEP_RATE = 0.3
DECAY_RATE = 0.01

F32 = jnp.float32
BF16 = jnp.bfloat16
NN = ((1,), (0,))
NT = ((1,), (1,))
TN = ((0,), (0,))
GELU_A = 0.044715
GELU_C = 0.7978845608028654


def dot(a, b, dims=NN):
    return lax.dot_general(a, b, (dims, ((), ())), preferred_element_type=F32)


def matrix_shapes():
    return [(D, 3 * D), (D, D), (D, FF), (FF, D), (D, 6 * D)]


def bias_lengths():
    return [3 * D, D, FF, D, 6 * D]


def owner_extents(groups):
    return [row_count // groups * col_count for row_count, col_count in matrix_shapes()]


def unpack(packed, bias_packed, groups):
    flattened = packed.reshape(groups, -1)
    matrices = []
    offset = 0
    for row_count, col_count in matrix_shapes():
        extent = row_count // groups * col_count
        matrices.append(flattened[:, offset : offset + extent].reshape(row_count, col_count))
        offset = offset + extent
    bias_rows = bias_packed.reshape(groups, -1)
    biases = []
    offset = 0
    for length in bias_lengths():
        extent = length // groups
        biases.append(bias_rows[:, offset : offset + extent].reshape(length))
        offset = offset + extent
    return (matrices, biases)


def pack(matrices, biases, groups):
    packed = jnp.concatenate([matrix.reshape(groups, -1) for matrix in matrices], axis=1).reshape(
        -1, 128
    )
    bias_packed = jnp.concatenate(
        [vector.reshape(groups, -1) for vector in biases], axis=1
    ).reshape(-1)
    return (packed, bias_packed)


def region_sums(values, groups):
    extents = owner_extents(groups)
    flattened = values.reshape(-1, sum(extents))
    totals = []
    offset = 0
    for extent in extents:
        totals.append(jnp.sum(flattened[:, offset : offset + extent]))
        offset = offset + extent
    return jnp.stack(totals)


def spread_ratio(ratio, groups):
    pieces = [
        jnp.broadcast_to(ratio[position], (extent,))
        for position, extent in enumerate(owner_extents(groups))
    ]
    return jnp.concatenate(pieces)


def lamb_step(master, moment_one, moment_two, grads, groups, combine):
    new_one = BETA_ONE * moment_one + (1.0 - BETA_ONE) * grads
    new_two = BETA_TWO * moment_two + (1.0 - BETA_TWO) * grads * grads
    update = new_one / (jnp.sqrt(new_two) + ADAM_EPS) + DECAY_RATE * master
    weight_sq, update_sq = combine(
        region_sums(master * master, groups), region_sums(update * update, groups)
    )
    weight_norm = jnp.sqrt(weight_sq)
    update_norm = jnp.sqrt(update_sq)
    ratio = weight_norm / (update_norm + NORM_EPS)
    owner_width = sum(owner_extents(groups))
    scaled = (update.reshape(-1, owner_width) * spread_ratio(ratio, groups)[None, :]).reshape(
        update.shape
    )
    new_master = master - STEP_RATE * scaled
    return (new_master, new_one, new_two, jnp.stack([weight_norm, update_norm, ratio]))


def adam_step(values, moment_one, moment_two, grads):
    new_one = BETA_ONE * moment_one + (1.0 - BETA_ONE) * grads
    new_two = BETA_TWO * moment_two + (1.0 - BETA_TWO) * grads * grads
    return (values - STEP_RATE * new_one / (jnp.sqrt(new_two) + ADAM_EPS), new_one, new_two)


def norm_totals(weight_part, update_part):
    return lax.psum((weight_part, update_part), "grp")


def mean_last(v):
    return jnp.sum(v, axis=-1, keepdims=True) * (1.0 / v.shape[-1])


def normalise(v):
    centered = v - mean_last(v)
    r = lax.rsqrt(mean_last(centered * centered) + NORM_EPS)
    return centered * r, r


def norm_back(e, n, r):
    return r * (e - mean_last(e) - n * mean_last(e * n))


def fold(v):
    return jnp.sum(v.reshape(v.shape[0] // 8, 8, v.shape[1]), axis=0)


def lanes_of(j, rows):
    lane = lax.broadcasted_iota(jnp.int32, (rows, 2 * HDIM), 1)
    return (lane >= HDIM) if j else (lane < HDIM)


def block_kernel(
    lat, og, mod, w_qkv, w_out, w_up, w_down, b_qkv, b_out, b_up, b_down,
    out_o, latg_o, gqkv_o, gout_o, gup_o, gdown_o, bqkv_o, bout_o, bup_o, bdown_o, dmod_o,
    nm1, q3, k3, v3, att, lse, datt, dpj, dqs, nm2, hid, dhid, db2, db1, dmid, acc,
):
    length = lat.shape[0]
    tile = 256
    tiles = length // tile
    shift1, scale1, gate1 = mod[0:1, :], mod[1:2, :] + 1.0, mod[2:3, :]
    shift2, scale2, gate2 = mod[3:4, :], mod[4:5, :] + 1.0, mod[5:6, :]

    def qkv_tile(t, _):
        rows = pl.ds(pl.multiple_of(t * tile, tile), tile)
        n, _r = normalise(lat[rows, :].astype(F32))
        normed = (n * scale1 + shift1).astype(BF16)
        nm1[rows, :] = normed
        proj = (dot(normed, w_qkv[...]) + b_qkv[...]).astype(BF16)
        for p in range(PAIRS):
            q3[p, rows, :] = proj[:, 128 * p : 128 * p + 128] * jnp.asarray(HDIM**-0.5, BF16)
            k3[p, rows, :] = proj[:, D + 128 * p : D + 128 * p + 128]
            v3[p, rows, :] = proj[:, 2 * D + 128 * p : 2 * D + 128 * p + 128]
        return 0

    lax.fori_loop(0, tiles, qkv_tile, 0)

    qb = 256

    def att_pair(i, _):
        p = i // (length // qb)
        rows = pl.ds(pl.multiple_of((i % (length // qb)) * qb, qb), qb)
        q = q3[p, rows, :]
        outs, stats = [], []
        for j in range(2):
            qj = jnp.where(lanes_of(j, qb), q, jnp.zeros_like(q))
            s = dot(qj, k3[p], NT)
            m = jnp.max(s, axis=-1, keepdims=True)
            e = jnp.exp(s - m)
            l = jnp.sum(e, axis=-1, keepdims=True)
            outs.append(dot((e * (1.0 / l)).astype(BF16), v3[p]))
            stats.append(m + jnp.log(l))
        att[p, rows, :] = jnp.where(lanes_of(0, qb), outs[0], outs[1]).astype(BF16)
        lane = lax.broadcasted_iota(jnp.int32, (qb, 128), 1)
        lse[p, rows, :] = jnp.where(lane == 0, stats[0], stats[1])
        return 0

    lax.fori_loop(0, PAIRS * (length // qb), att_pair, 0)

    acc[...] = jnp.zeros_like(acc)

    def mlp_tile(t, _):
        rows = pl.ds(pl.multiple_of(t * tile, tile), tile)
        at = jnp.concatenate([att[p, rows, :] for p in range(PAIRS)], axis=1)
        branch1 = dot(at, w_out[...]) + b_out[...]
        mid = lat[rows, :].astype(F32) + gate1 * branch1
        n2, r2 = normalise(mid)
        normed = (n2 * scale2 + shift2).astype(BF16)
        nm2[rows, :] = normed
        pre = dot(normed, w_up[...]) + b_up[...]
        sq = pre * pre
        th = jnp.tanh(pre * (GELU_C + (GELU_C * GELU_A) * sq))
        half = 0.5 + 0.5 * th
        h = (pre * half).astype(BF16)
        hid[rows, :] = h
        slope = half + (0.5 * pre) * (1.0 - th * th) * (GELU_C + (3.0 * GELU_C * GELU_A) * sq)
        branch2 = dot(h, w_down[...]) + b_down[...]
        g = og[rows, :].astype(F32)
        out_o[rows, :] = (mid + gate2 * branch2).astype(BF16)
        d2 = (gate2 * g).astype(BF16)
        db2[rows, :] = d2
        dh = (dot(d2, w_down[...], NT) * slope).astype(BF16)
        dhid[rows, :] = dh
        dn2 = dot(dh, w_up[...], NT)
        dm = g + norm_back(dn2 * scale2, n2, r2)
        dmid[rows, :] = dm
        d1 = (gate1 * dm).astype(BF16)
        db1[rows, :] = d1
        da = dot(d1, w_out[...], NT).astype(BF16)
        for p in range(PAIRS):
            datt[p, rows, :] = da[:, 128 * p : 128 * p + 128]
        acc[2, :, 0:D] += fold(dm * branch1)
        acc[3, :, 0:D] += fold(dn2)
        acc[4, :, 0:D] += fold(dn2 * n2)
        acc[5, :, 0:D] += fold(g * branch2)
        acc[6, :, 0:D] += fold(d1.astype(F32))
        acc[7, :, 0:D] += fold(d2.astype(F32))
        acc[8, :, :] += fold(dh.astype(F32))
        return 0

    lax.fori_loop(0, tiles, mlp_tile, 0)

    def gmlp(c, _):
        cols = pl.ds(pl.multiple_of(c * D, D), D)
        gdown_o[cols, :] = dot(hid[:, cols], db2[...], TN)
        gup_o[:, cols] = dot(nm2[...], dhid[:, cols], TN)
        return 0

    lax.fori_loop(0, FF // D, gmlp, 0)
    for p in range(PAIRS):
        gout_o[128 * p : 128 * p + 128, :] = dot(att[p], db1[...], TN)

    kb = 256

    def att_back(p, _):
        stat = lse[p].T
        do = datt[p]
        q = q3[p]
        prod = (do.astype(F32) * att[p].astype(F32)).T
        keep = [lanes_of(j, length) for j in range(2)]
        dos = [jnp.where(keep[j], do, jnp.zeros_like(do)) for j in range(2)]
        qs = [jnp.where(keep[j], q, jnp.zeros_like(q)) for j in range(2)]
        inner = [
            jnp.sum(prod[HDIM * j : HDIM * j + HDIM, :], axis=0, keepdims=True) for j in range(2)
        ]
        dqs[...] = jnp.zeros_like(dqs)

        def keys(b, _):
            rows = pl.ds(pl.multiple_of(b * kb, kb), kb)
            k, v = k3[p, rows, :], v3[p, rows, :]
            dv, dk, dq = [], [], []
            for j in range(2):
                pt = jnp.exp(dot(k, qs[j], NT) - stat[j : j + 1, :])
                dst = (pt * (dot(v, dos[j], NT) - inner[j])).astype(BF16)
                dv.append(dot(pt.astype(BF16), dos[j]))
                dk.append(dot(dst, qs[j]))
                kj = jnp.where(lanes_of(j, kb), k, jnp.zeros_like(k))
                dq.append(dot(dst, kj, TN))
            dpj[2 * PAIRS + p, rows, :] = (dv[0] + dv[1]).astype(BF16)
            dpj[PAIRS + p, rows, :] = (dk[0] + dk[1]).astype(BF16)
            dqs[...] += dq[0] + dq[1]
            return 0

        lax.fori_loop(0, length // kb, keys, 0)
        dpj[p] = (dqs[...] * (HDIM**-0.5)).astype(BF16)
        return 0

    lax.fori_loop(0, PAIRS, att_back, 0)

    def last_tile(t, _):
        rows = pl.ds(pl.multiple_of(t * tile, tile), tile)
        dp = jnp.concatenate([dpj[c, rows, :] for c in range(3 * PAIRS)], axis=1)
        dn1 = dot(dp, w_qkv[...], NT)
        n1, r1 = normalise(lat[rows, :].astype(F32))
        latg_o[rows, :] = (dmid[rows, :] + norm_back(dn1 * scale1, n1, r1)).astype(BF16)
        acc[0, :, 0:D] += fold(dn1)
        acc[1, :, 0:D] += fold(dn1 * n1)
        acc[9, :, 0 : 3 * D] += fold(dp.astype(F32))
        return 0

    lax.fori_loop(0, tiles, last_tile, 0)
    for c in range(3):
        cols = jnp.concatenate([dpj[PAIRS * c + p] for p in range(PAIRS)], axis=1)
        gqkv_o[:, D * c : D * c + D] = dot(nm1[...], cols, TN)

    def total(i):
        return jnp.sum(acc[i], axis=0, keepdims=True)

    for i in range(6):
        dmod_o[i : i + 1, :] = total(i)[:, 0:D]
    bout_o[...] = total(6)[:, 0:D]
    bdown_o[...] = total(7)[:, 0:D]
    bup_o[...] = total(8)
    bqkv_o[...] = total(9)[:, 0 : 3 * D]


def block(lat, og, mod, weights, biases):
    length = lat.shape[0]
    row = lambda n: jax.ShapeDtypeStruct((1, n), F32)
    act = jax.ShapeDtypeStruct((length, D), BF16)
    mat = lambda r, c: jax.ShapeDtypeStruct((r, c), F32)
    vm = lambda *shape: pltpu.VMEM(shape, BF16)
    return pl.pallas_call(
        block_kernel,
        out_shape=(
            act, act, mat(D, 3 * D), mat(D, D), mat(D, FF), mat(FF, D),
            row(3 * D), row(D), row(FF), row(D), jax.ShapeDtypeStruct((6, D), F32),
        ),
        in_specs=[pl.BlockSpec(memory_space=pltpu.VMEM)] * 11,
        out_specs=[pl.BlockSpec(memory_space=pltpu.VMEM)] * 11,
        scratch_shapes=[
            vm(length, D), vm(PAIRS, length, 128), vm(PAIRS, length, 128), vm(PAIRS, length, 128),
            vm(PAIRS, length, 128), pltpu.VMEM((PAIRS, length, 128), F32), vm(PAIRS, length, 128),
            vm(3 * PAIRS, length, 128), pltpu.VMEM((length, 128), F32),
            vm(length, D), vm(length, FF), vm(length, FF), vm(length, D), vm(length, D),
            pltpu.VMEM((length, D), F32), pltpu.VMEM((10, 8, FF), F32),
        ],
        compiler_params=pltpu.CompilerParams(vmem_limit_bytes=60 << 20),
        name="block",
    )(lat, og, mod, *weights, *biases)


def local(
    latents, condition, out_grad, master, moment_one, moment_two, bias_master, bias_one, bias_two
):
    groups = lax.axis_size("grp")
    packed, bias_packed = (
        lax.all_gather(master.astype(BF16), "grp", axis=0, tiled=True),
        lax.all_gather(bias_master.astype(BF16), "grp", axis=0, tiled=True),
    )
    matrices, biases = unpack(packed, bias_packed, groups)
    w_ada = matrices[4]
    rows = [vector.astype(F32)[None, :] for vector in biases]
    cond_low = jax.nn.silu(condition).astype(BF16)
    modulation = jnp.dot(cond_low, w_ada, preferred_element_type=F32) + rows[4]
    (
        block_out, latent_grad, g_qkv, g_out, g_up, g_down, gb_qkv, gb_out, gb_up, gb_down, dmod,
    ) = block(latents, out_grad, modulation.reshape(6, D), matrices[:4], rows[:4])
    modulation_grad = dmod.reshape(1, 6 * D).astype(BF16)
    grad_ada = cond_low.T.astype(F32) * modulation_grad.astype(F32)
    grad_b_ada = modulation_grad.astype(F32)[0]
    silu_back = jax.vjp(jax.nn.silu, condition)[1]
    condition_grad = silu_back(jnp.dot(modulation_grad, w_ada.T, preferred_element_type=F32))[0]
    grad_pack, bias_pack = pack(
        [g_qkv, g_out, g_up, g_down, grad_ada],
        [gb_qkv[0], gb_out[0], gb_up[0], gb_down[0], grad_b_ada],
        groups,
    )
    summed, bias_summed = lax.psum((grad_pack, bias_pack), "rep")
    owned, bias_owned = (
        lax.psum_scatter(summed, "grp", scatter_dimension=0, tiled=True),
        lax.psum_scatter(bias_summed, "grp", scatter_dimension=0, tiled=True),
    )
    new_master, new_one, new_two, lamb_stats = lamb_step(
        master, moment_one, moment_two, owned, groups, norm_totals
    )
    new_bias, new_bias_one, new_bias_two = adam_step(bias_master, bias_one, bias_two, bias_owned)
    return (
        block_out,
        latent_grad,
        condition_grad,
        lamb_stats,
        new_master,
        new_one,
        new_two,
        new_master.astype(BF16),
        new_bias,
        new_bias_one,
        new_bias_two,
        new_bias.astype(BF16),
    )


def solution(mesh):
    row, own, vec = P(("rep", "grp"), None), P("grp", None), P("grp")
    return jax.shard_map(
        local,
        mesh=mesh,
        in_specs=(row, row, row, own, own, own, vec, vec, vec),
        out_specs=(row, row, row, P(), own, own, own, own, vec, vec, vec, vec),
        check_vma=False,
    )
```

profile of v0, /device:TPU:0, one launch (start us, length us, event | category | flops | bytes accessed | tf_op | source)
XLA Modules:
  0.0 472.3 jit_solution(5556464942012974500)
XLA Ops:
  7.3 2.9 convert_element_type.117
  11.9 12.6 %all-reduce = bf16[5760]{0:T(1024)(128)(2,1)S(1)} all-reduce(bf16[5760]{0:T(1024)(128)(2,1)S(1)} %dynamic-update-slice), channel_id=1, replica_groups=mesh['rep'=8,'grp'=4] {'grp'}, use_global_device_ids=true, to_apply=%add | all-reduce | flops 5760 | bytes 23040
  27.9 4.2 copy.23
  32.0 21.9 %all-gather.2.cloned.1.call-done = bf16[20736,128]{1,0:T(8,128)(2,1)} async-done(((bf16[5184,128]{1,0:T(8,128)(2,1)}), bf16[20736,128]{1,0:T(8,128)(2,1)}) %all-gather.2.cloned.1.call-update) | async-done | bytes 5308432 | tf_op jit(solution)/shard_map/all_gather | solution.py:341
  53.9 6.8 %reshape.181 = bf16[4,663552]{1,0:T(4,128)(2,1)} reshape(bf16[20736,128]{1,0:T(8,128)(2,1)} %all-gather.2.cloned.1.call-done) | data formatting | bytes 10616832 | tf_op jit(solution)/shard_map/reshape | solution.py:49
  60.7 2.5 copy-done.1
  65.0 2.9 reshape.182
  72.9 3.3 reshape.187.w_up
  78.0 64.5 %block.1 = (bf16[1024,384]{1,0:T(8,128)(2,1)}, bf16[1024,384]{1,0:T(8,128)(2,1)}, f32[384,1152]{1,0:T(8,128)}, f32[384,384]{1,0:T(8,128)}, f32[384,1536]{1,0:T(8...) custom-call(bf16[1024,384]{1,0:T(8,128)(2,1)} %lat.1, ...), custom_call_target="tpu_custom_call" | custom-call | tf_op jit(solution)/shard_map/block/pallas_call | solution.py:316
  147.2 4.7 reshape.192
  151.9 2.8 reshape.193
  157.7 2.7 constant_dynamic-update-slice_fusion.1
  163.5 2.5 multiply_dynamic-update-slice_fusion
  166.0 15.2 %reshape.194 = f32[20736,128]{1,0:T(8,128)} reshape(f32[4,663552]{1,0:T(4,128)} %multiply_dynamic-update-slice_fusion) | data formatting | bytes 21233664 | tf_op jit(solution)/shard_map/reshape | solution.py:67
  181.3 86.2 %reduce-scatter.2.cloned.1.call-done = f32[5184,128]{1,0:T(8,128)} async-done(((f32[20736,128]{1,0:T(8,128)}), f32[5184,128]{1,0:T(8,128)}) %reduce-scatter.2.cloned.1.call-update) | async-done | bytes 2654224 | tf_op jit(solution)/shard_map/reduce_scatter | solution.py:364
  268.8 118.4 %all-reduce.5.cloned.1.call-done = f32[5184,128]{1,0:T(8,128)} async-done(((f32[5184,128]{1,0:T(8,128)}), f32[5184,128]{1,0:T(8,128)}) %all-reduce.5.cloned.1.call-update) | async-done | bytes 2654224 | tf_op jit(solution)/shard_map/psum | solution.py:362
  387.2 7.4 %fusion.7 = (f32[5184,128]{1,0:T(8,128)S(1)}, f32[5184,128]{1,0:T(8,128)}, f32[5184,128]{1,0:T(8,128)}, f32[5184,128]{1,0:T(8,128)S(1)}) fusion(f32[5184,128]{1,0:T(8,128)S(1)} %copy-done, f32[5184,128]{1,0:T(8,128)} %all-reduce.5.cloned.1.call-done, f32[5184,128]{1,0:T(8,128)} %param.14, f32[5184,128]{1,0:T(8,128)} %param.13), kind=kLoop, calls=%fused_computation.48 | loop fusion | flops 7962624 | bytes 21233664 | tf_op jit(solution)/shard_map/mul | solution.py:100
  399.1 2.4 slice_reduce_fusion
  408.3 3.3 stack.60
  411.6 3.3 stack.53
  414.9 2.6 fusion.3
  417.5 10.3 %all-reduce.2 = (f32[5]{0:T(128)S(1)}, f32[5]{0:T(128)S(1)}, f32[5760]{0:T(1024)S(1)}) all-reduce(f32[5]{0:T(128)S(1)} %stack.60, f32[5]{0:T(128)S(1)} %stack.53, f32[5760]{0:T(1024)S(1)} %reshape.196), channel_id=1, replica_groups=mesh['rep'=8,'grp'=4] {'grp'}, use_global_device_ids=true, to_apply=%region_13.14 | all-reduce | flops 5770 | bytes 46160 | tf_op jit(solution)/shard_map/psum | solution.py:120
  430.1 20.7 %psum.33 = f32[1440]{0:T(1024)S(1)} all-reduce(f32[1440]{0:T(1024)S(1)} %dynamic-slice.2), channel_id=1, replica_groups=mesh['rep'=8,'grp'=4] {'rep'}, use_global_device_ids=true, to_apply=%region_14.15 | all-reduce | flops 1440 | bytes 11520 | tf_op jit(solution)/shard_map/psum | solution.py:362
  458.0 6.7 %fusion.10 = (bf16[5184,128]{1,0:T(8,128)(2,1)}, f32[5184,128]{1,0:T(8,128)}) fusion(f32[5184,128]{1,0:T(8,128)S(1)} %copy-done, f32[5184,128]{1,0:T(8,128)} %bitcast.52, f32[5184,128]{1,0:T(8,128)} %get-tuple-element.49, f32[5184,128]{1,0:T(8,128)} %get-tuple-element.48), kind=kLoop, calls=%fused_computation.50 | loop fusion | flops 5308416 | bytes 14598144 | tf_op jit(solution)/shard_map/convert_element_type | solution.py:379
  (106 shorter events, 45.8 us)
Async XLA Ops:
  7.2 3.1 copy-start.13
  7.2 3.1 copy-start.7
  7.2 20.3 %copy-start.8 = (f32[1,384]{1,0:T(1,128)S(1)}, f32[1,384]{1,0:T(1,128)}, u32[]{:S(2)}) copy-start(f32[1,384]{1,0:T(1,128)} %param.10) | copy-start | bytes 4612
  7.2 46.7 %all-gather.2.cloned.1.call-start = ((), (), s32[]{:S(2)}) async-start(), calls=%async_computation.1 | async-start | bytes 6635520 | tf_op jit(solution)/shard_map/all_gather | solution.py:341
  10.2 257.2 %reduce-scatter.2.cloned.1.call-start = ((), (), s32[]{:S(2)}) async-start(), calls=%async_computation.2 | async-start | bytes 13271040 | tf_op jit(solution)/shard_map/reduce_scatter | solution.py:364
  60.7 2.5 copy-start.1
  60.7 4.3 slice-start
  65.0 5.4 %slice-start.1 = ((bf16[4,663552]{1,0:T(4,128)(2,1)}), bf16[4,110592]{1,0:T(4,128)(2,1)S(1)}, s32[]{:S(2)}) async-start(bf16[4,663552]{1,0:T(4,128)(2,1)} %reshape.181), calls=%async_computation.5 | async-start | bytes 1769472 | tf_op jit(solution)/shard_map/slice | solution.py:54
  68.0 4.1 slice-start.2
  69.9 6.4 %copy-start.3 = (bf16[4,147456]{1,0:T(4,128)(2,1)S(1)}, bf16[4,147456]{1,0:T(4,128)(2,1)}, u32[]{:S(2)}) copy-start(bf16[4,147456]{1,0:T(4,128)(2,1)} %get-tuple-element.53) | copy-start | bytes 3538948
  144.8 1.3 copy-start.5
  151.9 2.8 copy-start.6
  160.4 2.9 copy-start.2
  160.4 3.1 copy-start.4
  181.1 87.1 %copy-start.12 = (f32[1,1152]{1,0:T(1,128)S(1)}, f32[1,1152]{1,0:T(1,128)}, u32[]{:S(2)}) copy-start(f32[1,1152]{1,0:T(1,128)} %get-tuple-element.30) | copy-start | bytes 13828
  181.2 87.2 %copy-start.15 = (f32[1,384]{1,0:T(1,128)S(1)}, f32[1,384]{1,0:T(1,128)}, u32[]{:S(2)}) copy-start(f32[1,384]{1,0:T(1,128)} %get-tuple-element.31) | copy-start | bytes 4612
  181.2 87.3 %copy-start.11 = (f32[1,1536]{1,0:T(1,128)S(1)}, f32[1,1536]{1,0:T(1,128)}, u32[]{:S(2)}) copy-start(f32[1,1536]{1,0:T(1,128)} %get-tuple-element.32) | copy-start | bytes 18436
  181.2 87.3 %copy-start.14 = (f32[1,384]{1,0:T(1,128)S(1)}, f32[1,384]{1,0:T(1,128)}, u32[]{:S(2)}) copy-start(f32[1,384]{1,0:T(1,128)} %get-tuple-element.33) | copy-start | bytes 4612
  181.2 206.0 %copy-start = (f32[5184,128]{1,0:T(8,128)S(1)}, f32[5184,128]{1,0:T(8,128)}, u32[]{:S(2)}) copy-start(f32[5184,128]{1,0:T(8,128)} %param.12) | copy-start | bytes 7962628
  181.2 206.0 %all-reduce.5.cloned.1.call-start = ((), (), s32[]{:S(2)}) async-start(), calls=%async_computation.3 | async-start | bytes 5308416 | tf_op jit(solution)/shard_map/psum | solution.py:362
  458.0 6.7 %copy-start.9 = (f32[1440]{0:T(1024)S(1)}, f32[1440]{0:T(1024)}, u32[]{:S(2)}) copy-start(f32[1440]{0:T(1024)} %param.16) | copy-start | bytes 17284
  458.0 6.7 %copy-start.10 = (f32[1440]{0:T(1024)S(1)}, f32[1440]{0:T(1024)}, u32[]{:S(2)}) copy-start(f32[1440]{0:T(1024)} %param.17) | copy-start | bytes 17284
Sparse Core Ops, SparseCore 0:
  10.3 43.5 all-gather.1
  181.3 86.1 reduce-scatter.1
  271.1 116.0 all-reduce.4
where the time goes:
time: 481 us; the launch traced here: 472 us
  waiting for transfers between devices  227 us (47%)
  local copies, waits for them, and re-layouts  82.6 us (17%)
  Pallas kernels  64.5 us (13%)
  blocking collectives  43.6 us (9%)
  other arithmetic  34.6 us (7%)
  between operations  15.8 us (3%)
    psum x1, waiting for transfers between devices, local(): summed, bias_summed = lax.psum((grad_pack, bias_pack), 'rep')  118 us
    reduce_scatter x1, waiting for transfers between devices, local(): lax.psum_scatter(summed, 'grp', scatter_dimension=0, tiled=True)  86.2 us
    pallas_call x1, Pallas kernels, block(): pl.pallas_call(block_kernel, out_shape=(act, act, mat(D, 3 * D), mat(D, D...  64.5 us
    unnamed x48, local copies, waits for them, and re-layouts  24.1 us
    all_gather x1, waiting for transfers between devices, local(): lax.all_gather(master.astype(BF16), 'grp', axis=0, tiled=True)  21.9 us
    psum x1, blocking collectives, local(): summed, bias_summed = lax.psum((grad_pack, bias_pack), 'rep')  20.7 us
    reshape x1, local copies, waits for them, and re-layouts, pack(): jnp.concatenate([matrix.reshape(groups, -1) for matrix in matrices], axis=1)  15.2 us
    reduce_sum x8, other arithmetic, region_sums(): totals.append(jnp.sum(flattened[:, offset:offset + extent]))  13.6 us
  transfers between devices with their start and end apart: 3, of which 3 were waited for; matrix products, arithmetic and copies ran while one was open for 2% of the time, Pallas kernels for 0%

commit v1 on v0

v1 whole, which is shorter than its diff:
```python
import math

import jax
import jax.numpy as jnp
from jax import lax
from jax.experimental import pallas as pl
from jax.experimental.pallas import tpu as pltpu
from jax.sharding import PartitionSpec as P

D = 384
FF = 1536
HEADS = 6
HDIM = 64
PAIRS = HEADS // 2

NORM_EPS = 1e-06
BETA_ONE = 0.5
BETA_TWO = 0.5
ADAM_EPS = 1e-06
STEP_RATE = 0.3
DECAY_RATE = 0.01

F32 = jnp.float32
BF16 = jnp.bfloat16
NN = ((1,), (0,))
NT = ((1,), (1,))
TN = ((0,), (0,))
GELU_A = 0.044715
GELU_C = 0.7978845608028654


def dot(a, b, dims=NN):
    return lax.dot_general(a, b, (dims, ((), ())), preferred_element_type=F32)


def matrix_shapes():
    return [(D, 3 * D), (D, D), (D, FF), (FF, D), (D, 6 * D)]


def bias_lengths():
    return [3 * D, D, FF, D, 6 * D]


def owner_extents(groups):
    return [row_count // groups * col_count for row_count, col_count in matrix_shapes()]


def mean_last(v):
    return jnp.sum(v, axis=-1, keepdims=True) * (1.0 / v.shape[-1])


def normalise(v):
    centered = v - mean_last(v)
    r = lax.rsqrt(mean_last(centered * centered) + NORM_EPS)
    return centered * r, r


def norm_back(e, n, r):
    return r * (e - mean_last(e) - n * mean_last(e * n))


def fold(v):
    return jnp.sum(v.reshape(v.shape[0] // 8, 8, v.shape[1]), axis=0)


def lanes_of(j, rows):
    lane = lax.broadcasted_iota(jnp.int32, (rows, 2 * HDIM), 1)
    return (lane >= HDIM) if j else (lane < HDIM)


def regions(groups):
    found, base = [], 0
    for (row_count, col_count), extent in zip(matrix_shapes(), owner_extents(groups)):
        found.append((base, extent // 128, col_count // 128, row_count // groups))
        base += extent // 128
    return found


class Chunk:
    def __init__(self, kind, name, stride, row0, rows, col0, cols, plan, pair=None):
        self.kind, self.name, self.stride, self.row0, self.rows = kind, name, stride, row0, rows
        self.col0, self.cols, self.pair, self.half, self.unit = col0, cols, pair, rows // 2, plan.unit
        self.slabs = rows * cols // (2 * plan.unit * 128)
        self.per = -(-self.slabs // plan.layers)
        self.sets = self.slabs // self.per
        self.direct = pair is not None

    def slab(self, s):
        tiles = self.cols // 128
        return self.unit * (s // tiles), 128 * (s % tiles)

    def tile(self, s):
        col = self.slab(s)[1] // 128
        return self.col0 // 128 + col if self.pair is None else col * PAIRS + self.pair


def adam(first, second, grad):
    first = BETA_ONE * first + (1.0 - BETA_ONE) * grad
    second = BETA_TWO * second + (1.0 - BETA_TWO) * grad * grad
    return first / (second * lax.rsqrt(second) + ADAM_EPS), first, second


class Plan:
    def __init__(self, groups, reps, length):
        self.groups, self.reps, self.length = groups, reps, length
        self.layers = reps // 2
        self.regions = regions(groups)
        self.rows = sum(r[1] for r in self.regions)
        part = D // groups
        self.unit = part // 2
        self.chunks = []
        for i in range(2):
            rows = FF // groups // 2
            self.chunks.append(Chunk(3, "gdown", FF // groups, rows * i, rows, 0, D, self))
        for i in range(2):
            self.chunks.append(Chunk(2, "gup", part, 0, part, FF // 2 * i, FF // 2, self))
        self.chunks.append(Chunk(1, "gout", part, 0, part, 0, D, self))
        for p in range(PAIRS):
            self.chunks.append(Chunk(0, "gq", part, 0, part, 0, D, self, p))
        self.biases = [n // groups for n in bias_lengths()]
        self.widths = [128 * groups + 4 * D + 2 * D + FF, 3 * D, 2 * D]


def scratch_of(plan):
    length, groups, layers = plan.length, plan.groups, plan.layers
    b = lambda *shape: pltpu.VMEM(shape, BF16)
    f = lambda *shape: pltpu.VMEM(shape, F32)
    dma = lambda *shape: pltpu.SemaphoreType.DMA(shape)
    n = len(plan.chunks)
    items = dict(
        lat=b(length, D), og=b(length, D),
        w_qkv=b(D, 3 * D), w_out=b(D, D), w_up=b(D, FF), w_down=b(FF, D), w_ada=b(D // groups, 6 * D),
        mst=f(plan.rows, 128), one=f(plan.rows, 128), two=f(plan.rows, 128), gpk=f(plan.rows, 128),
        act_s=f(groups, 1, 128), act_r=f(groups, 1, 128),
        mp_s=f(groups, 1, 6 * D), mp_r=f(groups, 1, 6 * D), mod=f(1, 6 * D),
        b_all=f(groups, 1, sum(plan.biases)), b_qkv=f(1, 3 * D), b_out=f(1, D), b_up=f(1, FF), b_down=f(1, D),
        nm1=b(length, D), q3=b(PAIRS, length, 128), k3=b(PAIRS, length, 128), v3=b(PAIRS, length, 128),
        att=b(PAIRS, length, 128), lse=f(PAIRS, 8, length), datt=b(PAIRS, length, 128),
        dpj=b(3 * PAIRS * length, 128), dqs=f(length, 128), stt=f(4, length),
        hid=b(length, FF), dhid=b(length, FF),
        dmid=f(length, D), acc=f(10, 8, FF),
        gdown=f(FF, D), gup=f(D, FF), gout=f(D, D), gq=f(PAIRS, D, D),
        rows2=f(32, 128 + 6 * D), brow=f(1, 6 * D + sum(bias_lengths()[:4])),
        bg=f(groups, 1, sum(plan.biases)),
        cg_s=f(groups, 1, 128), cg_r=f(groups, 1, 128), nrm=f(groups, 1, 128),
        ls=dma(16), ws=dma(6, 3), wr=dma(6, 3), ts=dma(5, 3), tr=dma(5, 3),
        es=dma(n, 2 * layers), cs=dma(n, 7), cr=dma(n, 7), xs=dma(3, 5), xr=dma(3, 5), os=dma(16), st=dma(5, 3),
    )
    for i, width in enumerate(plan.widths):
        items[f"row{i}"] = f(groups, 2, layers, 1, width)
    kinds = {BF16: b, F32: f}
    for k, one in enumerate(plan.chunks):
        items[f"ra{k}"] = f(2, one.rows, one.cols)
        items[f"sb{k}"] = b(one.rows, one.cols)
        items[f"rb{k}"] = b(one.rows, one.cols)
        if not one.direct:
            items[f"sc{k}"] = kinds[HALF_TYPE](one.half, one.cols)
            items[f"rc{k}"] = kinds[HALF_TYPE](one.half, one.cols)
        halves = 2 if one.direct else 1
        items[f"hf{k}"] = f(halves * one.slabs, plan.unit, 128)
        if LAYER_TYPE is not F32:
            items[f"sd{k}"] = b(halves * one.slabs, plan.unit, 128)
        items[f"rd{k}"] = kinds[LAYER_TYPE](halves * layers, one.per, plan.unit, 128)
        items[f"ag{k}"] = kinds[SPREAD_TYPE](2, one.slabs, plan.unit, 128)
    return items


HALF_TYPE, LAYER_TYPE, SPREAD_TYPE = BF16, BF16, BF16


def encode(value):
    return (value * jnp.abs(value)).astype(BF16)


def decode(code):
    wide = code.astype(F32)
    return wide * lax.rsqrt(jnp.maximum(jnp.abs(wide), 1e-37))


class Refs:
    def __init__(self, names, refs):
        for name, ref in zip(names, refs, strict=True):
            setattr(self, name, ref)


ARGS = ["lat_h", "og_h", "cond", "mst_h", "one_h", "two_h", "bm_h"]
OUTS = ["out_h", "latg_h", "gpk_h", "none_h", "ntwo_h", "back", "squares", "bgrad"]


def at(value, step):
    return pl.multiple_of(value, step)


def step_kernel(plan, names, *refs):
    v = Refs(ARGS + OUTS + names, refs)
    groups, reps, layers, length = plan.groups, plan.reps, plan.layers, plan.length
    r, g = lax.axis_index("rep"), lax.axis_index("grp")
    h, zi, c, x = r % 2, r // 2, g % 2, g // 2
    g1, g2, g3, r1 = g + 1 - 2 * c, g + 2 - 4 * x, 3 - g, r + 1 - 2 * h
    others = [g1, g2, g3]
    part = D // groups

    def rdma(src, dst, send, recv, rep, grp):
        return pltpu.make_async_remote_copy(
            src_ref=src, dst_ref=dst, send_sem=send, recv_sem=recv,
            device_id=(rep, grp), device_id_type=pl.DeviceIdType.MESH,
        )

    def layer_rep(dz):
        return ((zi + dz) % layers) * 2 + h

    barrier = pltpu.get_barrier_semaphore()

    def greet(rep, grp):
        pl.semaphore_signal(barrier, inc=1, device_id=(rep, grp), device_id_type=pl.DeviceIdType.MESH)

    for t in others:
        greet(r, t)

    def any_rep(d):
        return ((zi + d // 2) % layers) * 2 + (h + d) % 2

    def greet_rep(d, _):
        greet(any_rep(d), g)
        return 0

    lax.fori_loop(1, reps, greet_rep, 0)

    def region_copy(src, dst, k, sem):
        base, count, _, _ = plan.regions[k]
        return pltpu.make_async_copy(src.at[pl.ds(base, count), :], dst.at[pl.ds(base, count), :], sem)

    loads = [region_copy(v.mst_h, v.mst, k, v.ls.at[k]) for k in range(5)]
    for k in (0, 4):
        loads[k].start()
    lat_in = pltpu.make_async_copy(v.lat_h, v.lat, v.ls.at[5])
    og_in = pltpu.make_async_copy(v.og_h, v.og, v.ls.at[6])
    one_in = pltpu.make_async_copy(v.one_h, v.one, v.ls.at[7])
    two_in = pltpu.make_async_copy(v.two_h, v.two, v.ls.at[8])
    lat_in.start()
    for k in (1, 2, 3):
        loads[k].start()

    cond = v.cond[...]
    sig = 1.0 / (1.0 + jnp.exp(-cond))
    act = (cond * sig).astype(BF16).astype(F32)
    v.act_s[...] = jnp.zeros_like(v.act_s)
    for j in range(groups):
        v.act_s[j, :, 0:part] = act[:, part * j : part * j + part]
    v.b_all[g] = v.bm_h[...].reshape(1, sum(plan.biases)).astype(BF16).astype(F32)

    def own(k, dst, first, place=lambda t: t):
        base, _, tiles, rows = plan.regions[k]
        for i in range(rows // part):
            for t in range(tiles):
                piece = v.mst[pl.ds(base + part * i * tiles + t, part, stride=tiles), :]
                dst[pl.ds(at(first + part * i, 32), part), 128 * place(t) : 128 * place(t) + 128] = piece.astype(BF16)

    mats = [v.w_qkv] * PAIRS + [v.w_out, v.w_up, v.w_down]
    kinds = [0] * PAIRS + [1, 2, 3]

    def pair_place(t):
        return (t % PAIRS) * 3 + t // PAIRS

    def weight_copy(k, route):
        rows = plan.regions[kinds[k]][3]
        block, to = [(g, g1), (g, g2), (g2, g1)][route]
        where = pl.ds(at(block * rows, 32), rows)
        ref = mats[k].at[where, D * k : D * k + D] if k < PAIRS else mats[k].at[where, :]
        return rdma(ref, ref, v.ws.at[k, route], v.wr.at[k, route], r, to)

    loads[0].wait()
    own(0, v.w_qkv, g * part, pair_place)
    pl.semaphore_wait(barrier, 3 + reps - 1)

    def to_others(kind, src, dst):
        return [
            rdma(src(t), dst, v.ts.at[kind, i], v.tr.at[kind, i], r, t) for i, t in enumerate(others)
        ]

    act_out = to_others(0, lambda t: v.act_s.at[t], v.act_r.at[g])
    bias_out = to_others(1, lambda t: v.b_all.at[g], v.b_all.at[g])
    mod_out = to_others(2, lambda t: v.mp_s.at[t], v.mp_r.at[g])
    for copy in act_out:
        copy.start()
    weight_copy(0, 1).start()
    weight_copy(0, 0).start()
    v.act_r[g] = v.act_s[g]
    loads[4].wait()
    own(4, v.w_ada, 0)
    for copy in act_out:
        copy.wait_recv()
    left = jnp.concatenate([v.act_r[j][:, 0:part] for j in range(groups)] + [jnp.zeros((8 - groups, part), F32)], axis=0)
    parts = dot(left.astype(BF16), v.w_ada[...])
    for j in range(groups):
        v.mp_s[j] = parts[j : j + 1, :]
    for copy in mod_out:
        copy.start()
    v.mp_r[g] = v.mp_s[g]
    for p in range(1, PAIRS):
        weight_copy(p, 1).start()
        weight_copy(p, 0).start()
    for copy in bias_out:
        copy.start()
    og_in.start()
    for k in (1, 2, 3):
        loads[k].wait()
        own(k, mats[PAIRS - 1 + k], g * plan.regions[k][3])
        weight_copy(PAIRS - 1 + k, 1).start()
        weight_copy(PAIRS - 1 + k, 0).start()
        if k == 2:
            weight_copy(0, 1).wait_recv()
            weight_copy(0, 2).start()
    lat_in.wait()
    tile = 256
    tiles = length // tile

    def centre_tile(t, _):
        rows = pl.ds(at(t * tile, tile), tile)
        v.dmid[rows, :] = normalise(v.lat[rows, :].astype(F32))[0]
        return 0

    lax.fori_loop(0, tiles, centre_tile, 0)
    one_in.start()
    two_in.start()
    for copy in bias_out:
        copy.wait_recv()
    starts = [sum(plan.biases[:k]) for k in range(5)]

    def bias_row(k):
        s, n = starts[k], plan.biases[k]
        return jnp.concatenate([v.b_all[j][:, s : s + n] for j in range(groups)], axis=1)

    for k, ref in enumerate([v.b_qkv, v.b_out, v.b_up, v.b_down]):
        ref[...] = bias_row(k)
    flat = v.b_qkv[...]
    tiles_of = [flat[:, 128 * t : 128 * t + 128] for t in range(3 * PAIRS)]
    for t in range(3 * PAIRS):
        v.b_qkv[:, 128 * pair_place(t) : 128 * pair_place(t) + 128] = tiles_of[t]
    for copy in mod_out:
        copy.wait_recv()
    total = v.mp_r[0]
    for j in range(1, groups):
        total = total + v.mp_r[j]
    v.mod[...] = total + bias_row(4)

    def forward(k):
        weight_copy(k, 1).wait_recv()
        weight_copy(k, 2).start()

    def arrived(k):
        weight_copy(k, 0).wait_recv()
        weight_copy(k, 2).wait_recv()


    mod = v.mod
    shift1, scale1, gate1 = mod[:, 0:D], mod[:, D : 2 * D] + 1.0, mod[:, 2 * D : 3 * D]
    shift2, scale2, gate2 = mod[:, 3 * D : 4 * D], mod[:, 4 * D : 5 * D] + 1.0, mod[:, 5 * D : 6 * D]
    def norm_tile(t, _):
        rows = pl.ds(at(t * tile, tile), tile)
        v.nm1[rows, :] = (v.dmid[rows, :] * scale1 + shift1).astype(BF16)
        return 0

    lax.fori_loop(0, tiles, norm_tile, 0)

    def pair_cols(p):
        return pl.ds(at(p * D, D), D)

    def qkv_tile(p, t):
        rows = pl.ds(at(t * tile, tile), tile)
        proj = (dot(v.nm1[rows, :], v.w_qkv[:, pair_cols(p)]) + v.b_qkv[:, pair_cols(p)]).astype(BF16)
        v.q3[p, rows, :] = proj[:, 0:128] * jnp.asarray(HDIM**-0.5, BF16)
        v.k3[p, rows, :] = proj[:, 128:256]
        v.v3[p, rows, :] = proj[:, 256:384]

    qb = 256
    q_steps = length // qb

    def att_step(p, i):
        rows = pl.ds(at(i * qb, qb), qb)
        q = v.q3[p, rows, :]
        outs, stats = [], []
        for j in range(2):
            qj = jnp.where(lanes_of(j, qb), q, jnp.zeros_like(q))
            s = dot(qj, v.k3[p], NT)
            m = jnp.max(s, axis=-1, keepdims=True)
            e = jnp.exp(s - m)
            l = jnp.sum(e, axis=-1, keepdims=True)
            outs.append(dot((e * (1.0 / l)).astype(BF16), v.v3[p]))
            stats.append(m + jnp.log(l))
        v.att[p, rows, :] = jnp.where(lanes_of(0, qb), outs[0], outs[1]).astype(BF16)
        lane = lax.broadcasted_iota(jnp.int32, (qb, 128), 1)
        v.lse[p, :, rows] = jnp.where(lane == 0, stats[0], stats[1]).T[0:8, :]

    forwards = {(0, 0): [2], (0, 2): [3], (1, 2): [4], (2, 1): [5]}

    def att_pair(p, _):
        for k in range(PAIRS):
            @pl.when(p == k)
            def _(k=k):
                arrived(k)

        def project(t, _):
            qkv_tile(p, t)
            return 0

        lax.fori_loop(0, tiles, project, 0)

        @pl.when(p == 0)
        def _():
            forward(1)

        def attend(i, _):
            att_step(p, i)
            for (pp, ii), ks in forwards.items():
                @pl.when((p == pp) & (i == ii))
                def _(ks=ks):
                    for k in ks:
                        forward(k)
            return 0

        lax.fori_loop(0, q_steps, attend, 0)
        return 0

    lax.fori_loop(0, PAIRS, att_pair, 0)
    og_in.wait()
    for k in (3, 4, 5):
        arrived(k)

    acc = v.acc
    acc[...] = jnp.zeros_like(acc)

    def whole(i):
        return pl.ds(at(i * length, length), length)

    def spare_put(which, t, value):
        for i in range(PAIRS):
            v.dpj[pl.ds(at((which * PAIRS + i) * length + t * tile, tile), tile), :] = value[:, 128 * i : 128 * i + 128]

    def spare(which):
        return jnp.concatenate([v.dpj[whole(which * PAIRS + i), :] for i in range(PAIRS)], axis=1)

    def mlp_tile(t, _):
        rows = pl.ds(at(t * tile, tile), tile)
        atv = jnp.concatenate([v.att[p, rows, :] for p in range(PAIRS)], axis=1)
        branch1 = dot(atv, v.w_out[...]) + v.b_out[...]
        mid = v.lat[rows, :].astype(F32) + gate1 * branch1
        n2, r2 = normalise(mid)
        normed = (n2 * scale2 + shift2).astype(BF16)
        spare_put(0, t, normed)
        pre = dot(normed, v.w_up[...]) + v.b_up[...]
        sq = pre * pre
        th = jnp.tanh(pre * (GELU_C + (GELU_C * GELU_A) * sq))
        half = 0.5 + 0.5 * th
        hd = (pre * half).astype(BF16)
        v.hid[rows, :] = hd
        slope = half + (0.5 * pre) * (1.0 - th * th) * (GELU_C + (3.0 * GELU_C * GELU_A) * sq)
        branch2 = dot(hd, v.w_down[...]) + v.b_down[...]
        og = v.og[rows, :].astype(F32)
        v.og[rows, :] = (mid + gate2 * branch2).astype(BF16)
        d2 = (gate2 * og).astype(BF16)
        spare_put(1, t, d2)
        dh = (dot(d2, v.w_down[...], NT) * slope).astype(BF16)
        v.dhid[rows, :] = dh
        dn2 = dot(dh, v.w_up[...], NT)
        dm = og + norm_back(dn2 * scale2, n2, r2)
        v.dmid[rows, :] = dm
        d1 = (gate1 * dm).astype(BF16)
        spare_put(2, t, d1)
        da = dot(d1, v.w_out[...], NT).astype(BF16)
        for p in range(PAIRS):
            v.datt[p, rows, :] = da[:, 128 * p : 128 * p + 128]
        acc[2, :, 0:D] += fold(dm * branch1)
        acc[3, :, 0:D] += fold(dn2)
        acc[4, :, 0:D] += fold(dn2 * n2)
        acc[5, :, 0:D] += fold(og * branch2)
        acc[6, :, 0:D] += fold(d1.astype(F32))
        acc[7, :, 0:D] += fold(d2.astype(F32))
        acc[8, :, :] += fold(dh.astype(F32))
        return 0

    lax.fori_loop(0, tiles, mlp_tile, 0)
    out_copy = pltpu.make_async_copy(v.og, v.out_h, v.os.at[0])
    out_copy.start()

    def total_of(i, width):
        return jnp.sum(acc[i], axis=0, keepdims=True)[:, 0:width]

    def low_row(i):
        return total_of(i, D).astype(BF16).astype(F32)

    rowbufs = [v.row0, v.row1, v.row2]

    def row_put(n, pieces):
        ref, place = rowbufs[n].at[g, h, zi], 0
        for piece in pieces:
            ref[:, place : place + piece.shape[1]] = piece
            place += piece.shape[1]

    def row_copy(n, stage):
        ref = rowbufs[n]
        src, to = {
            1: (ref.at[g, h], (r1, g)), 2: (ref.at[g], (r, g2)), 3: (ref.at[g], (r, g1)), 4: (ref.at[g2], (r, g1)),
        }[stage]
        return rdma(src, src, v.xs.at[n, stage], v.xr.at[n, stage], *to)

    def row_wait(n, sems):
        few = rowbufs[n].at[g, h, pl.ds(0, layers - 1)]
        return pltpu.make_async_copy(few, few, sems.at[n, 0])

    def row_step(n, stage):
        if stage == 0:
            ref = rowbufs[n].at[g, h, zi]

            def send_row(dz, _):
                rdma(ref, ref, v.xs.at[n, 0], v.xr.at[n, 0], layer_rep(dz), g).start()
                return 0

            lax.fori_loop(1, layers, send_row, 0)
        elif stage == 1:
            row_wait(n, v.xr).wait()
            row_copy(n, 1).start()
        elif stage == 2:
            row_copy(n, 1).wait_recv()
            row_copy(n, 2).start()
            row_copy(n, 3).start()
        elif stage == 3:
            row_copy(n, 2).wait_recv()
            row_copy(n, 4).start()
        else:
            row_copy(n, 3).wait_recv()
            row_copy(n, 4).wait_recv()

    def row_sent(n):
        row_wait(n, v.xs).wait()
        for stage in (1, 2, 3, 4):
            row_copy(n, stage).wait_send()

    row_put(0, [v.act_s[j] for j in range(groups)] + [low_row(i) for i in range(2, 6)]
            + [total_of(6, D), total_of(8, FF), total_of(7, D)])
    row_step(0, 0)

    def grad_of(k):
        one = plan.chunks[k]
        return v.gq.at[one.pair] if one.pair is not None else getattr(v, one.name)

    def buf(k, *names):
        return [getattr(v, f"{name}{k}") for name in names]

    def copy_a(k, kk):
        one = plan.chunks[k]
        (ra,) = buf(k, "ra")
        rows = pl.ds(at((2 * kk + 1 - c) * one.stride + one.row0, 32), one.rows)
        src = grad_of(k).at[rows, one.col0 : one.col0 + one.cols]
        return rdma(src, ra.at[kk], v.cs.at[k, 5 + kk], v.cr.at[k, 5 + kk], r, g1)

    def copy_b(k):
        sb, rb = buf(k, "sb", "rb")
        return rdma(sb, rb, v.cs.at[k, 0], v.cr.at[k, 0], r, g2)

    def copy_c(k):
        sc, rc = buf(k, "sc", "rc")
        return rdma(sc, rc, v.cs.at[k, 1], v.cr.at[k, 1], r1, g)

    def copy_f(k):
        (ag,) = buf(k, "ag")
        return rdma(ag.at[h], ag.at[h], v.cs.at[k, 4], v.cr.at[k, 4], r1, g)

    def by_rows(rows, body):
        def run(i, _):
            body(at(i * plan.unit, 16))
            return 0

        lax.fori_loop(0, rows // plan.unit, run, 0)

    def rows_at(value):
        return pl.ds(at(value, 16), plan.unit)

    def s1(k):
        for kk in range(2):
            copy_a(k, kk).start()

    def s2(k):
        one = plan.chunks[k]
        ra, sb = buf(k, "ra", "sb")
        for kk in range(2):
            copy_a(k, kk).wait_recv()
        first = (2 * (1 - x) + c) * one.stride + one.row0
        cols = slice(one.col0, one.col0 + one.cols)

        def body(i):
            sb[rows_at(i), :] = encode(grad_of(k)[rows_at(first + i), cols] + ra[1 - x, rows_at(i), :])

        by_rows(one.rows, body)
        copy_b(k).start()

    def s3(k):
        one = plan.chunks[k]
        ra, rb, sc = buf(k, "ra", "rb", "sc")
        copy_b(k).wait_recv()
        first = (1 - h) * one.half
        cols = slice(one.col0, one.col0 + one.cols)

        def body(i):
            mine = grad_of(k)[rows_at(g * one.stride + one.row0 + first + i), cols]
            total = mine + ra[x, rows_at(first + i), :] + decode(rb[rows_at(first + i), :])
            sc[rows_at(i), :] = encode(total)

        by_rows(one.half, body)
        copy_c(k).start()

    def set_at(k, q):
        return pl.ds(q * plan.chunks[k].per, plan.chunks[k].per)

    def sent_slabs(k):
        return buf(k, "hf")[0] if LAYER_TYPE is F32 else buf(k, "sd")[0]

    def copy_d(k, q, to):
        (rd,) = buf(k, "rd")
        slot = (zi - to + layers) % layers
        return rdma(sent_slabs(k).at[set_at(k, q)], rd.at[slot], v.cs.at[k, 2], v.cr.at[k, 2], to * 2 + h, g)

    def s4(k):
        one = plan.chunks[k]
        ra, rb, rc, hf = buf(k, "ra", "rb", "rc", "hf")
        copy_c(k).wait_recv()
        first = h * one.half
        for s in range(one.slabs):
            i, col = one.slab(s)
            cols = slice(col, col + 128)
            near = pl.ds(at(first + i, 16), plan.unit)
            mine = grad_of(k)[rows_at(g * one.stride + one.row0 + first + i), one.col0 + col : one.col0 + col + 128]
            far = decode(rb[near, cols]) + decode(rc[i : i + plan.unit, cols])
            value = mine + ra[x, near, cols] + far
            hf[s] = value
            if LAYER_TYPE is not F32:
                buf(k, "sd")[0][s] = encode(value)
        for q in range(one.sets):
            to = (q + k) % layers

            @pl.when(to != zi)
            def _(q=q, to=to):
                copy_d(k, q, to).start()

    def mine_of(k):
        return (zi - k % layers + layers) % layers

    def slab_bytes(k, count, sem, name):
        if name == "ag":
            ref = buf(k, "ag")[0].at[0, pl.ds(0, count * plan.chunks[k].per)]
        else:
            ref = buf(k, "rd")[0].at[pl.ds(0, count)]
        return pltpu.make_async_copy(ref, ref, sem)

    def copy_e(k, q, dz):
        (ag,) = buf(k, "ag")
        ref = ag.at[h, set_at(k, q)]
        return rdma(ref, ref, v.es.at[k, dz], v.cr.at[k, 3], layer_rep(dz), g)

    def s5(k):
        one = plan.chunks[k]
        hf, rd, ag = buf(k, "hf", "rd", "ag")
        q, per = mine_of(k), one.per

        @pl.when(q < one.sets)
        def _():
            slab_bytes(k, layers - 1, v.cr.at[k, 2], "rd").wait()
            for i in range(per):
                def add(z, value):
                    return value + decode(rd[z, i])

                value = lax.fori_loop(1, layers, add, hf[q * per + i], unroll=layers <= 4)
                ag[h, q * per + i] = encode(value)

            def send(dz, _):
                copy_e(k, q, dz).start()
                return 0

            lax.fori_loop(1, layers, send, 0)

    def s6(k):
        sets = plan.chunks[k].sets

        @pl.when(mine_of(k) < sets)
        def _():
            slab_bytes(k, sets - 1, v.cr.at[k, 3], "ag").wait()

        @pl.when(mine_of(k) >= sets)
        def _():
            slab_bytes(k, sets, v.cr.at[k, 3], "ag").wait()

        copy_f(k).start()

    def s7(k):
        copy_f(k).wait_recv()
        unpack(k)

    def unpack(k):
        one = plan.chunks[k]
        (ag,) = buf(k, "ag")
        base, _, across, _ = plan.regions[one.kind]
        for half in range(2):
            for s in range(one.slabs):
                first = base + (one.row0 + half * one.half + one.slab(s)[0]) * across + one.tile(s)
                v.gpk[pl.ds(first, plan.unit, stride=across), :] = decode(ag[half, s])

    def sent(k):
        sets = plan.chunks[k].sets
        for kk in range(0 if k in (2, 3) else 2):
            copy_a(k, kk).wait_send()
        copy_b(k).wait_send()
        copy_c(k).wait_send()
        copy_f(k).wait_send()

        @pl.when(mine_of(k) < sets)
        def _():
            slab_bytes(k, sets - 1, v.cs.at[k, 2], "rd").wait()
            spread(k, layers - 1)

        @pl.when(mine_of(k) >= sets)
        def _():
            slab_bytes(k, sets, v.cs.at[k, 2], "rd").wait()

    def spread(k, count):
        def wait(dz, _):
            copy_e(k, mine_of(k), dz).wait_send()
            return 0

        lax.fori_loop(1, 1 + count, wait, 0)

    def direct_out(k, hh, q):
        sd, rd = buf(k, "sd", "rd")
        to = (q + k) % layers
        slot = ((zi - to + layers) % layers) * 2 + (h - hh) % 2
        src = sd.at[pl.ds((hh * plan.chunks[k].sets + q) * plan.chunks[k].per, plan.chunks[k].per)]
        return rdma(src, rd.at[slot], v.cs.at[k, 2], v.cr.at[k, 2], to * 2 + hh, g)

    def direct_back(k, d):
        (ag,) = buf(k, "ag")
        ref = ag.at[h, set_at(k, mine_of(k))]
        return rdma(ref, ref, v.es.at[k, d], v.cr.at[k, 3], any_rep(d), g)

    def d3(k):
        one = plan.chunks[k]
        ra, rb, hf, sd = buf(k, "ra", "rb", "hf", "sd")
        copy_b(k).wait_recv()
        for hh in range(2):
            for s in range(one.slabs):
                i, col = one.slab(s)
                i = i + hh * one.half
                cols = slice(col, col + 128)
                mine = grad_of(k)[rows_at(g * one.stride + one.row0 + i), one.col0 + col : one.col0 + col + 128]
                value = mine + ra[x, i : i + plan.unit, cols] + decode(rb[i : i + plan.unit, cols])
                hf[hh * one.slabs + s] = value
                sd[hh * one.slabs + s] = encode(value)
        for hh in range(2):
            for q in range(one.sets):
                @pl.when(((q + k) % layers != zi) | (hh != h))
                def _(hh=hh, q=q):
                    direct_out(k, hh, q).start()

    def d5(k):
        one = plan.chunks[k]
        hf, rd, ag = buf(k, "hf", "rd", "ag")
        q, per = mine_of(k), one.per

        @pl.when(q < one.sets)
        def _():
            slab_bytes(k, reps - 1, v.cr.at[k, 2], "rd").wait()
            for i in range(per):
                def add(d, value):
                    return value + decode(rd[d, i])

                value = lax.fori_loop(1, reps, add, hf[h * one.slabs + q * per + i], unroll=reps <= 8)
                ag[h, q * per + i] = encode(value)

            def send(d, _):
                direct_back(k, d).start()
                return 0

            lax.fori_loop(1, reps, send, 0)

    def d7(k):
        sets = plan.chunks[k].sets

        @pl.when(mine_of(k) < sets)
        def _():
            slab_bytes(k, 2 * sets - 1, v.cr.at[k, 3], "rd").wait()

        @pl.when(mine_of(k) >= sets)
        def _():
            slab_bytes(k, 2 * sets, v.cr.at[k, 3], "rd").wait()

        unpack(k)

    def direct_sent(k):
        sets = plan.chunks[k].sets
        for kk in range(2):
            copy_a(k, kk).wait_send()
        copy_b(k).wait_send()

        @pl.when(mine_of(k) < sets)
        def _():
            slab_bytes(k, 2 * sets - 1, v.cs.at[k, 2], "rd").wait()

            def wait(d, _):
                direct_back(k, d).wait_send()
                return 0

            lax.fori_loop(1, reps, wait, 0)

        @pl.when(mine_of(k) >= sets)
        def _():
            slab_bytes(k, 2 * sets, v.cs.at[k, 2], "rd").wait()

    direct_steps = {"1": s1, "2": s2, "3": d3, "5": d5, "7": d7}
    steps = dict(zip("1234567", (s1, s2, s3, s4, s5, s6, s7)))

    def run(text):
        for word in text:
            if word[0] == "r":
                row_step(int(word[1]), int(word[2]))
            else:
                k = int(word[1])
                (direct_steps if plan.chunks[k].direct else steps)[word[0]](k)

    def stores(k):
        pairs = ((v.gpk, v.gpk_h), (v.one, v.none_h), (v.two, v.ntwo_h))
        return [region_copy(a, b, k, v.st.at[k, i]) for i, (a, b) in enumerate(pairs)]

    def lamb(k):
        base, count, _, _ = plan.regions[k]

        size = 288

        def body(i, sums):
            rows = pl.ds(at(base + i * size, 32), size)
            grad, w = v.gpk[rows, :], v.mst[rows, :]
            move, v.one[rows, :], v.two[rows, :] = adam(v.one[rows, :], v.two[rows, :], grad)
            update = move + DECAY_RATE * w
            v.gpk[rows, :] = update
            return sums[0] + fold(w * w), sums[1] + fold(update * update)

        zero = jnp.zeros((8, 128), F32)
        sums = lax.fori_loop(0, count // size, body, (zero, zero))
        for copy in stores(k):
            copy.start()
        return [jnp.sum(jnp.sum(one, axis=1, keepdims=True), axis=0, keepdims=True) for one in sums]

    def g_down(i, _):
        cols = pl.ds(at(i * D, D), D)
        v.gdown[cols, :] = dot(v.hid[:, cols], spare(1), TN)
        return 0

    def g_up(i, _):
        cols = pl.ds(at(i * D, D), D)
        v.gup[:, cols] = dot(spare(0), v.dhid[:, cols], TN)
        return 0

    lax.fori_loop(0, FF // D, g_down, 0)
    run(["10", "11", "r01"])
    lax.fori_loop(0, FF // D // 2, g_up, 0)
    run(["20", "12"])
    lax.fori_loop(FF // D // 2, FF // D, g_up, 0)
    run(["21", "13"])
    for p in range(PAIRS):
        v.gout[128 * p : 128 * p + 128, :] = dot(v.att[p], spare(2), TN)
    run(["22", "14"])

    kb = 256
    k_steps = length // kb
    after = {
        0: ["23", "24"], 2: ["30"], 3: ["15", "31"], 4: ["25", "32", "40"], 5: ["33", "r02"],
        6: ["34", "41", "42"], 7: ["16", "35", "43", "50"], 8: ["26", "44", "51"],
        9: ["52", "55", "r03"], 10: ["53", "60"], 11: ["17", "36", "61", "62", "54"],
    }

    def att_back(it, _):
        p, b = it // k_steps, it % k_steps
        do, q = v.datt[p], v.q3[p]

        @pl.when(b == 0)
        def _():
            prod = (do.astype(F32) * v.att[p].astype(F32)).T
            v.stt[0:2, :] = v.lse[p, 0:2, :]
            for j in range(2):
                v.stt[2 + j : 3 + j, :] = jnp.sum(prod[HDIM * j : HDIM * j + HDIM, :], axis=0, keepdims=True)
            v.dqs[...] = jnp.zeros_like(v.dqs)

        rows = pl.ds(at(b * kb, kb), kb)
        kk, vv = v.k3[p, rows, :], v.v3[p, rows, :]
        dv, dk, dq = [], [], []
        for j in range(2):
            keep = lanes_of(j, length)
            dos = jnp.where(keep, do, jnp.zeros_like(do))
            qs = jnp.where(keep, q, jnp.zeros_like(q))
            pt = jnp.exp(dot(kk, qs, NT) - v.stt[j : j + 1, :])
            dst = (pt * (dot(vv, dos, NT) - v.stt[2 + j : 3 + j, :])).astype(BF16)
            dv.append(dot(pt.astype(BF16), dos))
            dk.append(dot(dst, qs))
            kj = jnp.where(lanes_of(j, kb), kk, jnp.zeros_like(kk))
            dq.append(dot(dst, kj, TN))
        v.dpj[pl.ds(at((2 * PAIRS + p) * length + b * kb, kb), kb), :] = (dv[0] + dv[1]).astype(BF16)
        v.dpj[pl.ds(at((PAIRS + p) * length + b * kb, kb), kb), :] = (dk[0] + dk[1]).astype(BF16)
        v.dqs[...] += dq[0] + dq[1]

        @pl.when(b == k_steps - 1)
        def _():
            v.dpj[whole(p), :] = (v.dqs[...] * (HDIM**-0.5)).astype(BF16)
            cols = jnp.concatenate([v.dpj[whole(i * PAIRS + p), :] for i in range(3)], axis=1)
            v.gq[p] = dot(v.nm1[...], cols, TN)
            acc[9, :, pair_cols(p)] = fold(cols.astype(F32))

        for i, text in after.items():
            @pl.when(it == i)
            def _(text=text):
                run(text)
        return 0

    lax.fori_loop(0, PAIRS * k_steps, att_back, 0)

    row_put(1, [total_of(9, 3 * D)])
    row_step(1, 0)

    for k in (2, 3):
        for kk in range(2):
            copy_a(k, kk).wait_send()

    def last_tile(t, _):
        rows = pl.ds(at(t * tile, tile), tile)
        order = [k * PAIRS + p for p in range(PAIRS) for k in range(3)]
        dp = jnp.concatenate([v.dpj[pl.ds(at(i * length + t * tile, tile), tile), :] for i in order], axis=1)
        dn1 = dot(dp, v.w_qkv[...], NT)
        n1, _r = normalise(v.lat[rows, :].astype(F32))
        v.gup[0:tile, pair_cols(t)] = dn1
        acc[0, :, 0:D] += fold(dn1)
        acc[1, :, 0:D] += fold(dn1 * n1)
        for i, text in {0: ["27", "70", "r04"], 1: ["r11", "63"], 2: ["75"], 3: ["71", "72", "r12", "64", "56"]}.items():
            @pl.when(t == i)
            def _(text=text):
                run(text)
        return 0

    lax.fori_loop(0, tiles, last_tile, 0)
    row_put(2, [low_row(0), low_row(1)])
    run(["r20", "37"])

    def latent_tile(t, _):
        rows = pl.ds(at(t * tile, tile), tile)
        n1, rs1 = normalise(v.lat[rows, :].astype(F32))
        v.lat[rows, :] = (v.dmid[rows, :] + norm_back(v.gup[0:tile, pair_cols(t)] * scale1, n1, rs1)).astype(BF16)
        return 0

    lax.fori_loop(0, tiles, latent_tile, 0)
    latg_copy = pltpu.make_async_copy(v.lat, v.latg_h, v.os.at[11])
    latg_copy.start()

    one_in.wait()
    two_in.wait()
    sums = [None] * 5
    run(["r21", "r13"])
    sums[3] = lamb(3)
    run(["73"])
    sums[2] = lamb(2)
    run(["57", "r22", "r14", "74"])
    sums[1] = lamb(1)
    run(["76", "r23", "77", "r24"])

    m0 = 128 * groups
    base, _, across, _ = plan.regions[4]
    v.brow[...] = jnp.zeros_like(v.brow)

    def rows_of(n, _):
        sums = v.brow[...]
        for i in range(32):
            j = n * 32 + i
            early, mid, late = [ref.at[j // (2 * layers), (j // layers) % 2, j % layers] for ref in rowbufs]
            v.rows2[i : i + 1, 0:128] = early[:, pl.ds(at(g * 128, 128), 128)]
            dmod = jnp.concatenate([late[...], early[:, m0 : m0 + 4 * D]], axis=1)
            v.rows2[i : i + 1, 128:] = dmod
            sums = sums + jnp.concatenate([dmod, mid[...], early[:, m0 + 4 * D :]], axis=1)
        v.brow[...] = sums
        acts = v.rows2[:, 0:128].astype(BF16)
        for t in range(across):
            piece = dot(acts, v.rows2[:, 128 * t + 128 : 128 * t + 256].astype(BF16), TN)[0:part, :]
            rows = pl.ds(base + t, part, stride=across)
            v.gpk[rows, :] = v.gpk[rows, :] + piece
        return 0

    v.gpk[base : base + part * across, :] = jnp.zeros((part * across, 128), F32)
    lax.fori_loop(0, reps * groups // 32, rows_of, 0)

    dm4 = jnp.concatenate(
        [
            jnp.concatenate([v.row2[j, h, zi], v.row0[j, h, zi][:, m0 : m0 + 4 * D]], axis=1) for j in range(groups)
        ] + [jnp.zeros((8 - groups, 6 * D), F32)], axis=0
    )
    dact = dot(dm4.astype(BF16), v.w_ada[...], NT)
    v.cg_s[...] = jnp.zeros_like(v.cg_s)
    for j in range(groups):
        v.cg_s[j, :, 0:part] = dact[j : j + 1, :]
    cg_out = to_others(3, lambda t: v.cg_s.at[t], v.cg_r.at[g])
    for copy in cg_out:
        copy.start()
    v.cg_r[g] = v.cg_s[g]

    sums[4] = lamb(4)
    sums[0] = lamb(0)
    lane = lax.broadcasted_iota(jnp.int32, (1, 128), 1)
    packed = jnp.zeros((1, 128), F32)
    for k in range(5):
        packed = jnp.where(lane == k, sums[k][0], packed)
        packed = jnp.where(lane == 8 + k, sums[k][1], packed)
    v.nrm[g] = packed
    nrm_out = to_others(4, lambda t: v.nrm.at[g], v.nrm.at[g])
    for copy in nrm_out:
        copy.start()

    sumrow = v.brow[...]
    flat = sumrow[:, 6 * D : 9 * D]
    qkv_row = jnp.concatenate(
        [flat[:, 128 * pair_place(t) : 128 * pair_place(t) + 128] for t in range(3 * PAIRS)], axis=1
    )
    rest = sumrow[:, 9 * D :]
    grads_of = [qkv_row, rest[:, 0:D], rest[:, D : D + FF], rest[:, D + FF :], sumrow[:, 0 : 6 * D]]
    for j in range(groups):
        v.bg[j] = jnp.concatenate([one[:, n * j : n * j + n] for one, n in zip(grads_of, plan.biases)], axis=1)
    v.bgrad[...] = v.bg[g]

    for copy in cg_out:
        copy.wait_recv()
    back = jnp.concatenate([v.cg_r[j][:, 0:part] for j in range(groups)], axis=1)
    v.back[...] = back

    for copy in nrm_out:
        copy.wait_recv()
    squares = v.nrm[0]
    for j in range(1, groups):
        squares = squares + v.nrm[j]
    v.squares[...] = squares

    for k in range(6):
        for route in range(3):
            weight_copy(k, route).wait_send()
    for copy in act_out + bias_out + mod_out + cg_out + nrm_out:
        copy.wait_send()
    for k, one in enumerate(plan.chunks):
        (direct_sent if one.direct else sent)(k)
    for n in range(3):
        row_sent(n)
    out_copy.wait()
    latg_copy.wait()
    for k in range(5):
        for copy in stores(k):
            copy.wait()


def finish_kernel(plan, refs_in, refs_out, scratch):
    out_i, latg_i, upd, one, two, back, squares, bgrad, cond, mst, bm, b1, b2 = refs_in
    out_o, latg_o, condg, stats, nmst, none, ntwo, ncpy, nb, nb1, nb2, nbc = refs_out
    upd_v, mst_v, one_v, two_v, cpy_v, out_v, latg_v, scales, sem_in, sem_out, sem_b = scratch
    size = plan.regions[0][1]
    blocks = plan.rows // size

    def part(i):
        return pl.ds(at(i * size, 32), size)

    def load(i):
        pairs = ((upd, upd_v), (mst, mst_v))
        return [pltpu.make_async_copy(a.at[part(i), :], b.at[part(i), :], sem_in.at[i, n]) for n, (a, b) in enumerate(pairs)]

    def store(i):
        pairs = ((mst_v, nmst), (cpy_v, ncpy))
        return [pltpu.make_async_copy(a.at[part(i), :], b.at[part(i), :], sem_out.at[i, n]) for n, (a, b) in enumerate(pairs)]

    moves = [(one, one_v, none), (two, two_v, ntwo), (out_i, out_v, out_o), (latg_i, latg_v, latg_o)]
    arrive = [pltpu.make_async_copy(a, b, sem_b.at[n]) for n, (a, b, _c) in enumerate(moves)]
    leave = [pltpu.make_async_copy(b, d, sem_b.at[4 + n]) for n, (_a, b, d) in enumerate(moves)]
    for copy in arrive[0:1]:
        copy.start()
    for i in range(blocks):
        for copy in load(i):
            copy.start()
    for copy in arrive[1:]:
        copy.start()

    norms = jnp.sqrt(squares[...])
    weight_norm, update_norm = norms[:, 0:5], norms[:, 8:13]
    ratio = weight_norm / (update_norm + NORM_EPS)
    stats[0:1, :] = weight_norm
    stats[1:2, :] = update_norm
    stats[2:3, :] = ratio
    for k in range(5):
        scales[k] = jnp.broadcast_to(ratio[:, k : k + 1], (8, 128))
    sig = 1.0 / (1.0 + jnp.exp(-cond[...]))
    condg[...] = back[...] * (sig * (1.0 + cond[...] * (1.0 - sig)))
    move, first, second = adam(b1[...], b2[...], bgrad[...].reshape(bm.shape))
    fresh = bm[...] - STEP_RATE * move
    nb[...] = fresh
    nb1[...] = first
    nb2[...] = second
    nbc[...] = fresh.astype(BF16)

    arrive[0].wait()
    leave[0].start()
    edges = [base for base, _, _, _ in plan.regions] + [plan.rows]
    for i in range(blocks):
        for copy in load(i):
            copy.wait()
        for k in range(5):
            low, high = max(edges[k], i * size), min(edges[k + 1], (i + 1) * size)
            if low < high:
                scale = jnp.broadcast_to(scales[k][0:1, :], (96, 128))

                def apply(n, _, low=low, scale=scale):
                    rows = pl.ds(at(low + n * 96, 32), 96)
                    value = mst_v[rows, :] - STEP_RATE * (scale * upd_v[rows, :])
                    mst_v[rows, :] = value
                    cpy_v[rows, :] = value.astype(BF16)
                    return 0

                lax.fori_loop(0, (high - low) // 96, apply, 0)
        for copy in store(i):
            copy.start()
    for n in (1, 2, 3):
        arrive[n].wait()
        leave[n].start()
    for copy in leave:
        copy.wait()
    for i in range(blocks):
        for copy in store(i):
            copy.wait()


def local(
    latents, condition, out_grad, master, moment_one, moment_two, bias_master, bias_one, bias_two
):
    groups, reps = lax.axis_size("grp"), lax.axis_size("rep")
    plan = Plan(groups, reps, latents.shape[0])
    items = scratch_of(plan)
    names = list(items)
    sds = jax.ShapeDtypeStruct
    full = lambda dtype: sds(master.shape, dtype)
    count = bias_master.shape[0]
    act = sds(latents.shape, BF16)
    hbm, vmem = pl.BlockSpec(memory_space=pl.ANY), pl.BlockSpec(memory_space=pltpu.VMEM)
    held = pl.pallas_call(
        lambda *refs: step_kernel(plan, names, *refs),
        out_shape=(act, act, full(F32), full(F32), full(F32), sds((1, D), F32), sds((1, 128), F32), sds((1, count), F32)),
        in_specs=[hbm, hbm, vmem, hbm, hbm, hbm, vmem],
        out_specs=[hbm] * 5 + [vmem] * 3,
        scratch_shapes=list(items.values()),
        compiler_params=pltpu.CompilerParams(
            vmem_limit_bytes=67043328, collective_id=0, has_side_effects=True
        ),
        name="step",
    )(latents, out_grad, condition, master, moment_one, moment_two, bias_master)
    blocks = plan.rows // plan.regions[0][1]
    line = lambda dtype: sds((count,), dtype)
    f = lambda *shape: pltpu.VMEM(shape, F32)
    return pl.pallas_call(
        lambda *refs: finish_kernel(plan, refs[:13], refs[13:25], refs[25:]),
        out_shape=(
            act, act, sds(condition.shape, F32), sds((3, 5), F32),
            full(F32), full(F32), full(F32), full(BF16), line(F32), line(F32), line(F32), line(BF16),
        ),
        in_specs=[hbm] * 5 + [vmem] * 4 + [hbm] + [vmem] * 3,
        out_specs=[hbm, hbm, vmem, vmem, hbm, hbm, hbm, hbm, vmem, vmem, vmem, vmem],
        scratch_shapes=[
            f(plan.rows, 128), f(plan.rows, 128), f(plan.rows, 128), f(plan.rows, 128),
            pltpu.VMEM((plan.rows, 128), BF16), pltpu.VMEM(latents.shape, BF16), pltpu.VMEM(latents.shape, BF16),
            f(5, 8, 128), pltpu.SemaphoreType.DMA((blocks, 2)), pltpu.SemaphoreType.DMA((blocks, 2)),
            pltpu.SemaphoreType.DMA((8,)),
        ],
        compiler_params=pltpu.CompilerParams(vmem_limit_bytes=67043328),
        name="finish",
    )(*held, condition, master, bias_master, bias_one, bias_two)


def solution(mesh):
    row, own, vec = P(("rep", "grp"), None), P("grp", None), P("grp")
    return jax.shard_map(
        local,
        mesh=mesh,
        in_specs=(row, row, row, own, own, own, vec, vec, vec),
        out_specs=(row, row, row, P(), own, own, own, own, vec, vec, vec, vec),
        check_vma=False,
    )
```

time: 481 us -> 122 us (0.25); the launches traced: 472 us -> 121 us
  waiting for transfers between devices: 227 us -> 0 us
  local copies, waits for them, and re-layouts: 82.6 us -> 0 us
  Pallas kernels: 64.5 us -> 121 us
  blocking collectives: 43.6 us -> 0 us
  other arithmetic: 34.6 us -> 0 us
  between operations: 15.8 us -> 0.65 us
    psum x1 -> x0, waiting for transfers between devices: 118 us -> none  [local(): summed, bias_summed = lax.psum((grad_pack, bias_pack), 'rep')]
    reduce_scatter x1 -> x0, waiting for transfers between devices: 86.2 us -> none  [local(): lax.psum_scatter(summed, 'grp', scatter_dimension=0, tiled=True)]
    pallas_call x1 -> x2, Pallas kernels: 64.5 us -> 121 us  [the longest x1 112 us: local(): pl.pallas_call(lambda *refs: step_kernel(plan, names, *refs), out_shape=(...]
    reshape x14 -> x0, local copies, waits for them, and re-layouts: 44 us -> none  [the longest x1 15.2 us: pack(): jnp.concatenate([matrix.reshape(groups, -1) for matrix in matrices], axis=1)]
    psum x2 -> x0, blocking collectives: 31 us -> none  [the longest x1 20.7 us: local(): summed, bias_summed = lax.psum((grad_pack, bias_pack), 'rep')]
    unnamed x48 -> x0, local copies, waits for them, and re-layouts: 24.1 us -> none
    all_gather x1 -> x0, waiting for transfers between devices: 21.9 us -> none  [local(): lax.all_gather(master.astype(BF16), 'grp', axis=0, tiled=True)]
    reduce_sum x8 -> x0, other arithmetic: 13.6 us -> none  [region_sums(): totals.append(jnp.sum(flattened[:, offset:offset + extent]))]
  transfers between devices with their start and end apart: 3 -> 0, of which waited for: 3 -> 0; matrix products, arithmetic and copies ran while one was open for 2% -> 0% of each run, Pallas kernels for 0% -> 0%
where the time goes in v1:
time: 122 us; the launch traced here: 121 us
  Pallas kernels  121 us (99%)
    pallas_call x1, Pallas kernels, local(): pl.pallas_call(lambda *refs: step_kernel(plan, names, *refs), out_shape=(...  112 us
    pallas_call x1, Pallas kernels, local(): pl.pallas_call(lambda *refs: finish_kernel(plan, refs[:13], refs[13:25],...  8.91 us

profile of v1, /device:TPU:0, one launch (start us, length us, event | category | flops | bytes accessed | tf_op | source)
XLA Modules:
  0.0 121.4 jit_solution(6883858561327174854)
XLA Ops:
  0.6 111.8 %step.1 = (bf16[1024,384]{1,0:T(8,128)(2,1)}, bf16[1024,384]{1,0:T(8,128)(2,1)}, f32[5184,128]{1,0:T(8,128)}, f32[5184,128]{1,0:T(8,128)}, f32[5184,128]{1,0:T(8...) custom-call(bf16[1024,384]{1,0:T(8,128)(2,1)} %refs_0_.1, bf16[1024,384]{1,0:T(8,128)(2,1)} %refs_1_.1, ...), custom_call_target="tpu_custom_call" | custom-call | tf_op jit(solution)/shard_map/step/pallas_call | solution.py:1147
  112.5 8.9 %finish.1 = (bf16[1024,384]{1,0:T(8,128)(2,1)}, bf16[1024,384]{1,0:T(8,128)(2,1)}, f32[1,384]{1,0:T(1,128)}, f32[3,5]{1,0:T(4,128)}, f32[5184,128]{1,0:T(8,128)}...) custom-call(bf16[1024,384]{1,0:T(8,128)(2,1)} %get-tuple-element.20., ...), custom_call_target="tpu_custom_call" | custom-call | tf_op jit(solution)/shard_map/finish/pallas_call | solution.py:1161

commit v2 on v1

--- a/solution.py
+++ b/solution.py
@@ -147,7 +147,7 @@
         es=dma(n, 2 * layers), cs=dma(n, 7), cr=dma(n, 7), xs=dma(3, 5), xr=dma(3, 5), os=dma(16), st=dma(5, 3),
     )
     for i, width in enumerate(plan.widths):
-        items[f"row{i}"] = f(groups, 2, layers, 1, width)
+        items[f"row{i}"] = f(groups, plan.reps, 1, width)
     kinds = {BF16: b, F32: f}
     for k, one in enumerate(plan.chunks):
         items[f"ra{k}"] = f(2, one.rows, one.cols)
@@ -281,7 +281,7 @@
     act_out = to_others(0, lambda t: v.act_s.at[t], v.act_r.at[g])
     bias_out = to_others(1, lambda t: v.b_all.at[g], v.b_all.at[g])
     mod_out = to_others(2, lambda t: v.mp_s.at[t], v.mp_r.at[g])
-    for copy in act_out:
+    for copy in act_out + bias_out:
         copy.start()
     weight_copy(0, 1).start()
     weight_copy(0, 0).start()
@@ -300,8 +300,6 @@
     for p in range(1, PAIRS):
         weight_copy(p, 1).start()
         weight_copy(p, 0).start()
-    for copy in bias_out:
-        copy.start()
     og_in.start()
     for k in (1, 2, 3):
         loads[k].wait()
@@ -492,49 +490,50 @@
     rowbufs = [v.row0, v.row1, v.row2]
 
     def row_put(n, pieces):
-        ref, place = rowbufs[n].at[g, h, zi], 0
+        ref, place = rowbufs[n].at[g, r], 0
         for piece in pieces:
             ref[:, place : place + piece.shape[1]] = piece
             place += piece.shape[1]
 
-    def row_copy(n, stage):
+    def row_spread(n, d):
+        ref = rowbufs[n].at[g, r]
+        return rdma(ref, ref, v.xs.at[n, 0], v.xr.at[n, 0], any_rep(d), g)
+
+    def row_wait(n, sems):
+        few = rowbufs[n].at[g, pl.ds(0, reps - 1)]
+        return pltpu.make_async_copy(few, few, sems.at[n, 0])
+
+    def row_copies(n):
         ref = rowbufs[n]
-        src, to = {
-            1: (ref.at[g, h], (r1, g)), 2: (ref.at[g], (r, g2)), 3: (ref.at[g], (r, g1)), 4: (ref.at[g2], (r, g1)),
-        }[stage]
-        return rdma(src, src, v.xs.at[n, stage], v.xr.at[n, stage], *to)
-
-    def row_wait(n, sems):
-        few = rowbufs[n].at[g, h, pl.ds(0, layers - 1)]
-        return pltpu.make_async_copy(few, few, sems.at[n, 0])
+        last = (ref.at[g], g3) if n == 2 else (ref.at[g2], g1)
+        pairs = [(ref.at[g], g1), (ref.at[g], g2), last]
+        return [rdma(src, src, v.xs.at[n, 1 + i], v.xr.at[n, 1 + i], r, to) for i, (src, to) in enumerate(pairs)]
 
     def row_step(n, stage):
+        copies = row_copies(n)
         if stage == 0:
-            ref = rowbufs[n].at[g, h, zi]
-
-            def send_row(dz, _):
-                rdma(ref, ref, v.xs.at[n, 0], v.xr.at[n, 0], layer_rep(dz), g).start()
+            def send_row(d, _):
+                row_spread(n, d).start()
                 return 0
 
-            lax.fori_loop(1, layers, send_row, 0)
+            lax.fori_loop(1, reps, send_row, 0)
         elif stage == 1:
             row_wait(n, v.xr).wait()
-            row_copy(n, 1).start()
-        elif stage == 2:
-            row_copy(n, 1).wait_recv()
-            row_copy(n, 2).start()
-            row_copy(n, 3).start()
-        elif stage == 3:
-            row_copy(n, 2).wait_recv()
-            row_copy(n, 4).start()
+            copies[1].start()
+            copies[0].start()
+            if n == 2:
+                copies[2].start()
+        elif stage == 2 and n < 2:
+            copies[1].wait_recv()
+            copies[2].start()
         else:
-            row_copy(n, 3).wait_recv()
-            row_copy(n, 4).wait_recv()
+            for copy in copies if n == 2 else [copies[0], copies[2]]:
+                copy.wait_recv()
 
     def row_sent(n):
         row_wait(n, v.xs).wait()
-        for stage in (1, 2, 3, 4):
-            row_copy(n, stage).wait_send()
+        for copy in row_copies(n):
+            copy.wait_send()
 
     row_put(0, [v.act_s[j] for j in range(groups)] + [low_row(i) for i in range(2, 6)]
             + [total_of(6, D), total_of(8, FF), total_of(7, D)])
@@ -828,6 +827,9 @@
         pairs = ((v.gpk, v.gpk_h), (v.one, v.none_h), (v.two, v.ntwo_h))
         return [region_copy(a, b, k, v.st.at[k, i]) for i, (a, b) in enumerate(pairs)]
 
+    def whole_sum(one):
+        return jnp.sum(jnp.sum(one, axis=1, keepdims=True), axis=0, keepdims=True)
+
     def lamb(k):
         base, count, _, _ = plan.regions[k]
 
@@ -845,7 +847,7 @@
         sums = lax.fori_loop(0, count // size, body, (zero, zero))
         for copy in stores(k):
             copy.start()
-        return [jnp.sum(jnp.sum(one, axis=1, keepdims=True), axis=0, keepdims=True) for one in sums]
+        return [whole_sum(one) for one in sums]
 
     def g_down(i, _):
         cols = pl.ds(at(i * D, D), D)
@@ -858,7 +860,7 @@
         return 0
 
     lax.fori_loop(0, FF // D, g_down, 0)
-    run(["10", "11", "r01"])
+    run(["10", "11"])
     lax.fori_loop(0, FF // D // 2, g_up, 0)
     run(["20", "12"])
     lax.fori_loop(FF // D // 2, FF // D, g_up, 0)
@@ -870,9 +872,9 @@
     kb = 256
     k_steps = length // kb
     after = {
-        0: ["23", "24"], 2: ["30"], 3: ["15", "31"], 4: ["25", "32", "40"], 5: ["33", "r02"],
+        0: ["23", "24"], 2: ["30"], 3: ["15", "31"], 4: ["25", "32", "40"], 5: ["33", "r01"],
         6: ["34", "41", "42"], 7: ["16", "35", "43", "50"], 8: ["26", "44", "51"],
-        9: ["52", "55", "r03"], 10: ["53", "60"], 11: ["17", "36", "61", "62", "54"],
+        9: ["52", "55", "r02"], 10: ["53", "60"], 11: ["17", "36", "61", "62", "54"],
     }
 
     def att_back(it, _):
@@ -935,7 +937,7 @@
         v.gup[0:tile, pair_cols(t)] = dn1
         acc[0, :, 0:D] += fold(dn1)
         acc[1, :, 0:D] += fold(dn1 * n1)
-        for i, text in {0: ["27", "70", "r04"], 1: ["r11", "63"], 2: ["75"], 3: ["71", "72", "r12", "64", "56"]}.items():
+        for i, text in {0: ["27", "70", "r03"], 1: ["r11", "63"], 2: ["75"], 3: ["71", "72", "64", "56"]}.items():
             @pl.when(t == i)
             def _(text=text):
                 run(text)
@@ -958,41 +960,63 @@
     one_in.wait()
     two_in.wait()
     sums = [None] * 5
-    run(["r21", "r13"])
     sums[3] = lamb(3)
-    run(["73"])
+    run(["r21", "73"])
     sums[2] = lamb(2)
-    run(["57", "r22", "r14", "74"])
-    sums[1] = lamb(1)
-    run(["76", "r23", "77", "r24"])
-
     m0 = 128 * groups
     base, _, across, _ = plan.regions[4]
     v.brow[...] = jnp.zeros_like(v.brow)
-
-    def rows_of(n, _):
-        sums = v.brow[...]
-        for i in range(32):
-            j = n * 32 + i
-            early, mid, late = [ref.at[j // (2 * layers), (j // layers) % 2, j % layers] for ref in rowbufs]
-            v.rows2[i : i + 1, 0:128] = early[:, pl.ds(at(g * 128, 128), 128)]
-            dmod = jnp.concatenate([late[...], early[:, m0 : m0 + 4 * D]], axis=1)
-            v.rows2[i : i + 1, 128:] = dmod
-            sums = sums + jnp.concatenate([dmod, mid[...], early[:, m0 + 4 * D :]], axis=1)
-        v.brow[...] = sums
-        acts = v.rows2[:, 0:128].astype(BF16)
-        for t in range(across):
-            piece = dot(acts, v.rows2[:, 128 * t + 128 : 128 * t + 256].astype(BF16), TN)[0:part, :]
+    v.gpk[base : base + part * across, :] = jnp.zeros((part * across, 128), F32)
+
+    def ada(late):
+        tiles_of = range(0, 2 * D // 128) if late else range(2 * D // 128, across)
+
+        def rows_of(n, _):
+            one_sum, two_sum = [], []
+            for i in range(32):
+                j = n * 32 + i
+                early, mid, end = [ref.at[j // reps, j % reps] for ref in rowbufs]
+                v.rows2[i : i + 1, 0:128] = early[:, pl.ds(at(g * 128, 128), 128)]
+                if late:
+                    v.rows2[i : i + 1, 128 : 128 + 2 * D] = end[...]
+                    one_sum.append(end[...])
+                    two_sum.append(mid[...])
+                else:
+                    v.rows2[i : i + 1, 128 + 2 * D :] = early[:, m0 : m0 + 4 * D]
+                    one_sum.append(early[:, m0 : m0 + 4 * D])
+                    two_sum.append(early[:, m0 + 4 * D :])
+            spans = ((0, 2 * D), (6 * D, 9 * D)) if late else ((2 * D, 6 * D), (9 * D, v.brow.shape[1]))
+            for (low, high), pieces in zip(spans, (one_sum, two_sum)):
+                v.brow[:, low:high] += sum(pieces[1:], pieces[0])
+            acts = v.rows2[:, 0:128].astype(BF16)
+            for t in tiles_of:
+                piece = dot(acts, v.rows2[:, 128 * t + 128 : 128 * t + 256].astype(BF16), TN)[0:part, :]
+                rows = pl.ds(base + t, part, stride=across)
+                v.gpk[rows, :] = v.gpk[rows, :] + piece
+            return 0
+
+        lax.fori_loop(0, reps * groups // 32, rows_of, 0)
+        total = [jnp.zeros((8, 128), F32)] * 2
+        for t in tiles_of:
             rows = pl.ds(base + t, part, stride=across)
-            v.gpk[rows, :] = v.gpk[rows, :] + piece
-        return 0
-
-    v.gpk[base : base + part * across, :] = jnp.zeros((part * across, 128), F32)
-    lax.fori_loop(0, reps * groups // 32, rows_of, 0)
+            w = v.mst[rows, :]
+            move, first, second = adam(v.one[rows, :], v.two[rows, :], v.gpk[rows, :])
+            update = move + DECAY_RATE * w
+            v.one[rows, :] = first
+            v.two[rows, :] = second
+            v.gpk[rows, :] = update
+            total = [total[0] + fold(w * w), total[1] + fold(update * update)]
+        return total
+
+    run(["57", "r12", "74"])
+    early_sums = ada(False)
+    sums[1] = lamb(1)
+    run(["76", "r13", "r22"])
+    late_sums = ada(True)
 
     dm4 = jnp.concatenate(
         [
-            jnp.concatenate([v.row2[j, h, zi], v.row0[j, h, zi][:, m0 : m0 + 4 * D]], axis=1) for j in range(groups)
+            jnp.concatenate([v.row2[j, r], v.row0[j, r][:, m0 : m0 + 4 * D]], axis=1) for j in range(groups)
         ] + [jnp.zeros((8 - groups, 6 * D), F32)], axis=0
     )
     dact = dot(dm4.astype(BF16), v.w_ada[...], NT)
@@ -1004,7 +1028,10 @@
         copy.start()
     v.cg_r[g] = v.cg_s[g]
 
-    sums[4] = lamb(4)
+    for copy in stores(4):
+        copy.start()
+    sums[4] = [whole_sum(a + b) for a, b in zip(early_sums, late_sums)]
+    run(["77"])
     sums[0] = lamb(0)
     lane = lax.broadcasted_iota(jnp.int32, (1, 128), 1)
     packed = jnp.zeros((1, 128), F32)

time: 122 us -> 116 us (0.951)
  Pallas kernels: 121 us -> 114 us
    pallas_call x1, Pallas kernels: 112 us -> 105 us  [local(): pl.pallas_call(lambda *refs: step_kernel(plan, names, *refs), out_shape=(...]
where the time goes in v2:
time: 116 us; the launch traced here: 115 us
  Pallas kernels  114 us (98%)
    pallas_call x1, Pallas kernels, local(): pl.pallas_call(lambda *refs: step_kernel(plan, names, *refs), out_shape=(...  105 us
    pallas_call x1, Pallas kernels, local(): pl.pallas_call(lambda *refs: finish_kernel(plan, refs[:13], refs[13:25],...  8.91 us

profile of v2, /device:TPU:0, one launch (start us, length us, event | category | flops | bytes accessed | tf_op | source)
XLA Modules:
  0.0 115.2 jit_solution(2000081052019771586)
XLA Ops:
  0.6 105.5 %step.1 = (bf16[1024,384]{1,0:T(8,128)(2,1)}, bf16[1024,384]{1,0:T(8,128)(2,1)}, f32[5184,128]{1,0:T(8,128)}, f32[5184,128]{1,0:T(8,128)}, f32[5184,128]{1,0:T(8...) custom-call(bf16[1024,384]{1,0:T(8,128)(2,1)} %refs_0_.1, bf16[1024,384]{1,0:T(8,128)(2,1)} %refs_1_.1, ...), custom_call_target="tpu_custom_call" | custom-call | tf_op jit(solution)/shard_map/step/pallas_call | solution.py:1174
  106.1 8.9 %finish.1 = (bf16[1024,384]{1,0:T(8,128)(2,1)}, bf16[1024,384]{1,0:T(8,128)(2,1)}, f32[1,384]{1,0:T(1,128)}, f32[3,5]{1,0:T(4,128)}, f32[5184,128]{1,0:T(8,128)}...) custom-call(bf16[1024,384]{1,0:T(8,128)(2,1)} %get-tuple-element.20., ...), custom_call_target="tpu_custom_call" | custom-call | tf_op jit(solution)/shard_map/finish/pallas_call | solution.py:1188
